TPU v7x, 256 devices: a whole 4x4x8 slice. The times are simulated.
256 devices in a mesh: ctx: 64 (over z, y, core), tp: 4 (over x).
Axes of the slice: x: 4, y: 4, z: 8, core: 2. Of those that a mesh axis runs over, the one named last changes fastest.
Arguments:
- projected: bfloat16 [8192, 4, 4640], P('ctx', 'tp'), may hold values from -6 to 6
- conv_weight: float32 [4, 4, 2560], P('tp'), may hold values from -3 to 3
- conv_bias: float32 [4, 2560], P('tp'), may hold values from -1.5 to 1.5
- step_bias: float32 [4, 32], P('tp'), may hold values from -1 to 0.5
- log_rates: float32 [4, 32], P('tp'), as said below
- norm_gain: float32 [4, 2048], P('tp'), may hold values from 0.1 to 1.9
- out_weight: bfloat16 [4, 2048, 4096], P('tp', 'ctx'), may hold values from -0.0625 to 0.0625
Outputs:
- mixed: bfloat16 [8192, 4096], P('ctx', 'tp')
Inputs may be any that keep to these rules, and one draw needn't show every extreme that they name: log_rates lies between log(0.3 / 8192) and log(1 / 25).
All inputs are finite; a program needn't handle non-finite values.
Results may differ from a plain program's by a relative error of at most 0.0058.
Values may be sent and summed in bfloat16 or wider, within the bound.
No kernel may reach another device: no remote copies, remote signals or barrier semaphores. Data moves between devices by JAX's collectives and lax.ppermute only.
A program may use at most 320 MiB of HBM per device.

v0:
```python
import jax
import jax.numpy as jnp
import numpy as np
from jax import lax
from jax.sharding import PartitionSpec as P

P_SIZE = 64
N = 256
KCONV = 4
SPAN = 128
GCH = 2048
GCONV = 2560
highest_precision = lax.Precision.HIGHEST


def from_behind(shard, axis, by):
    peers = lax.axis_size(axis)
    pairs = [(i, i + by) for i in range(peers) if 0 <= i + by < peers]
    return lax.ppermute(shard, axis, pairs)


def ssd_blocks(inputs_x, step_sizes, decay_rate, b_keys, c_keys, block_rows):
    row_count = inputs_x.shape[0]
    block_count = row_count // block_rows
    head_count = inputs_x.shape[1]
    head_width = inputs_x.shape[2]
    state_count = b_keys.shape[1]
    x_blocks = inputs_x.reshape(block_count, block_rows, head_count, head_width)
    step_blocks = step_sizes.reshape(block_count, block_rows, head_count)
    b_blocks = b_keys.reshape(block_count, block_rows, state_count)
    c_blocks = c_keys.reshape(block_count, block_rows, state_count)
    causal_mask = (jnp.arange(block_rows)[:, None] >= jnp.arange(block_rows)[None, :])[None]

    def advance(carried, pieces):
        x_block, step_block, b_block, c_block = pieces
        log_steps = step_block * decay_rate[None, :]
        running = jnp.cumsum(log_steps, axis=0)
        intersection = jnp.dot(c_block, b_block.T, preferred_element_type=jnp.float32)
        b_float = b_block.astype(jnp.float32)
        c_float = c_block.astype(jnp.float32)
        log_gaps = running.T[:, :, None] - running.T[:, None, :]
        factors = jnp.where(causal_mask, jnp.exp(jnp.where(causal_mask, log_gaps, 0.0)), 0.0)
        factors = factors * intersection[None] * step_block.T[:, None, :]
        within = jnp.einsum("hts,shp->thp", factors, x_block, precision=highest_precision)
        carried_part = (
            jnp.einsum("tn,hpn->thp", c_float, carried, precision=highest_precision)
            * jnp.exp(running)[:, :, None]
        )
        tail_weight = jnp.exp(running[-1][None, :] - running) * step_block
        weighted = x_block * tail_weight[:, :, None]
        updated = carried * jnp.exp(running[-1])[:, None, None] + jnp.einsum(
            "shp,sn->hpn", weighted, b_float, precision=highest_precision
        )
        return (updated, within + carried_part)

    initial = jnp.zeros((head_count, head_width, state_count), jnp.float32)
    final_state, outputs = lax.scan(advance, initial, (x_blocks, step_blocks, b_blocks, c_blocks))
    total_log = jnp.sum(step_sizes * decay_rate[None, :], axis=0)
    return (outputs.reshape(row_count, head_count, head_width), final_state, total_log)


def on_device(projected, conv_weight, conv_bias, step_bias, log_rates, norm_gain, out_weight):
    row_count = projected.shape[0]
    conv_input = projected[:, :, GCH : GCH + GCONV]
    rim_rows = from_behind(conv_input[row_count - (KCONV - 1) :], "ctx", 1)
    padded = jnp.concatenate([rim_rows, conv_input], axis=0).astype(jnp.float32)
    mixed_conv = conv_bias[None]
    for offset in range(KCONV):
        mixed_conv = mixed_conv + conv_weight[:, offset][None] * padded[offset : offset + row_count]
    activated = jax.nn.silu(mixed_conv).astype(jnp.bfloat16)
    values = activated[:, :, :GCH]
    key_rows = activated[:, :, GCH:]
    raw_steps = projected[:, :, GCH + GCONV :]
    decay_rate = -jnp.exp(log_rates)
    devices = lax.axis_size("ctx")
    shard_width = GCH // devices
    shard_heads = max(1, shard_width // P_SIZE)
    piece_width = shard_width // shard_heads
    head_table = (
        np.arange(devices)[:, None] * shard_width // P_SIZE + np.arange(shard_heads)[None, :]
    ).reshape(-1)
    spread_steps = jnp.take(raw_steps, jnp.asarray(head_table, jnp.int32), axis=2)
    local_values, local_steps = (
        lax.all_to_all(values, "ctx", split_axis=2, concat_axis=0, tiled=True),
        lax.all_to_all(spread_steps, "ctx", split_axis=2, concat_axis=0, tiled=True),
    )
    all_keys = lax.all_gather(key_rows, "ctx", axis=0, tiled=True)
    sequence = local_values.shape[0]
    first_head = lax.axis_index("ctx") * shard_width // P_SIZE
    bias_slice = lax.dynamic_slice_in_dim(step_bias[0], first_head, shard_heads)
    rate_slice = lax.dynamic_slice_in_dim(decay_rate[0], first_head, shard_heads)
    step_sizes = jax.nn.softplus(local_steps[:, 0].astype(jnp.float32) + bias_slice[None, :])
    outputs, final_state, total_log = ssd_blocks(
        local_values[:, 0].astype(jnp.float32).reshape(sequence, shard_heads, piece_width),
        step_sizes,
        rate_slice,
        all_keys[:, 0, :N],
        all_keys[:, 0, N:],
        4 * SPAN,
    )
    pieces_out = [outputs.reshape(sequence, shard_width).astype(jnp.bfloat16)]
    scanned = lax.all_to_all(
        jnp.stack(pieces_out, axis=1), "ctx", split_axis=0, concat_axis=2, tiled=True
    )
    gated = scanned.astype(jnp.float32) * jax.nn.silu(projected[:, :, :GCH].astype(jnp.float32))
    normed = (
        gated * lax.rsqrt(jnp.mean(gated * gated, axis=2, keepdims=True) + 1e-05) * norm_gain[None]
    ).astype(jnp.bfloat16)
    summed = jnp.einsum(
        "tgr,grd->td",
        normed,
        lax.all_gather(out_weight, "ctx", axis=1, tiled=True),
        preferred_element_type=jnp.float32,
    )
    shares = lax.psum_scatter(summed, "tp", scatter_dimension=1, tiled=True)
    return shares.astype(jnp.bfloat16)


def solution(mesh):
    return jax.shard_map(
        on_device,
        mesh=mesh,
        in_specs=(
            P("ctx", "tp", None),
            P("tp", None, None),
            P("tp", None),
            P("tp", None),
            P("tp", None),
            P("tp", None),
            P("tp", "ctx", None),
        ),
        out_specs=P("ctx", "tp"),
        check_vma=False,
    )
```

profile of v0, /device:TPU:1, one launch (start us, length us, event | category | flops | bytes accessed | tf_op | source)
XLA Modules:
  0.0 387.9 jit_solution(16653090227472884516)
XLA Ops:
  8.2 4.7 %collective-permute-start = (bf16[3,1,2560]{2,0,1:T(4,128)(2,1)S(1)}, bf16[3,1,2560]{2,0,1:T(4,128)(2,1)S(1)}, u32[]{:S(2)}, u32[]{:S(2)}) collective-permute-start(bf16[3,1,2560]{2,0,1:T(4,128)(2,1)S(1)} %copy.77), channel_id=1, source_target_pairs={{0,4},{4,8},{8,12},{12,16},{16,20},{20,24},{24,28},{28,32},{32,36}... | collective-permute-start | bytes 46088 | tf_op jit(solution)/shard_map/ppermute | solution.py:19
  16.9 13.5 %all-to-all-start = ((bf16[128,1,64]{0,1,2:T(2,128)(2,1)}), bf16[128,1,64]{0,1,2:T(2,128)(2,1)S(1)}, u32[]{:S(2)}, u32[]{:S(2)}) async-start(bf16[128,1,64]{0,1,2:T(2,128)(2,1)} %copy.66), calls=%async_computation | async-start | bytes 65536 | tf_op jit(solution)/shard_map/all_to_all | solution.py:85
  31.7 11.5 %reduce.12 = bf16[2048,128]{1,0:T(8,128)(2,1)S(1)} reduce(bf16[2048,1,128]{2,1,0:T(2,128)(2,1)S(1)} %bitcast.163, bf16[]{:T(256)} %broadcast.159), dimensions={1}, to_apply=%bitcast.98.reduce_sub_computation | reduce | bytes 1048578
  44.2 10.3 %all-to-all-start.1 = ((bf16[64,2,2048]{2,1,0:T(2,128)(2,1)}), bf16[64,2,2048]{2,1,0:T(2,128)(2,1)S(1)}, u32[]{:S(2)}, u32[]{:S(2)}) async-start(bf16[64,2,2048]{2,1,0:T(2,128)(2,1)} %reshape.445), calls=%async_computation.1 | async-start | bytes 1048576 | tf_op jit(solution)/shard_map/all_to_all | solution.py:84
  57.5 14.9 %all-to-all-done.1 = bf16[64,2,2048]{2,1,0:T(2,128)(2,1)S(1)} async-done(((bf16[64,2,2048]{2,1,0:T(2,128)(2,1)}), bf16[64,2,2048]{2,1,0:T(2,128)(2,1)S(1)}, u32[]{:S(2)}, u32[]{:S(2)}) %all-to-all-start.1) | async-done | bytes 524320 | tf_op jit(solution)/shard_map/all_to_all | solution.py:84
  74.1 2.7 copy.70
  76.8 26.9 %all-gather.3.cloned.1.call-done = bf16[8192,1,512]{2,0,1:T(8,128)(2,1)} async-done(((bf16[128,1,512]{2,0,1:T(8,128)(2,1)}), bf16[8192,1,512]{2,0,1:T(8,128)(2,1)}) %all-gather.3.cloned.1.call-update) | async-done | bytes 8388624 | tf_op jit(solution)/shard_map/all_gather | solution.py:87
  103.7 5.9 %fusion.41 = (bf16[8192,1,256]{2,0,1:T(8,128)(2,1)}, bf16[8192,1,256]{2,0,1:T(8,128)(2,1)}) fusion(bf16[8192,1,512]{2,0,1:T(8,128)(2,1)} %all-gather.3.cloned.1.call-done), kind=kLoop, calls=%fused_computation.76 | loop fusion | bytes 16777216 | tf_op jit(solution)/shard_map/slice | solution.py:98
  109.6 184.8 %while.14 = (s32[]{:T(128)}, f32[1,32,256]{2,1,0:T(8,128)S(1)}, bf16[16,512,1,32]{1,3,2,0:T(8,128)(2,1)S(1)}, f32[16,512,1]{1,0,2:T(8,128)S(1)}, f32[1]{0:T(128)...) while((s32[]{:T(128)}, f32[1,32,256]{2,1,0:T(8,128)S(1)}, ...), condition=%wide.region_3.4_spmd.clone.clone, body=%wide.region_0.0_spmd.clone.clone.sunk | while | flops 337266176 | bytes 4002620 | solution.py:57
  113.5 2.4 broadcast_multiply_fusion.2
  125.0 2.4 broadcast_multiply_fusion.2
  136.5 2.4 broadcast_multiply_fusion.2
  148.1 2.4 broadcast_multiply_fusion.2
  159.7 2.5 broadcast_multiply_fusion.2
  171.3 2.4 broadcast_multiply_fusion.2
  182.8 2.4 broadcast_multiply_fusion.2
  194.4 2.4 broadcast_multiply_fusion.2
  206.0 2.4 broadcast_multiply_fusion.2
  217.5 2.4 broadcast_multiply_fusion.2
  229.1 2.4 broadcast_multiply_fusion.2
  240.6 2.4 broadcast_multiply_fusion.2
  252.1 2.4 broadcast_multiply_fusion.2
  263.7 2.4 broadcast_multiply_fusion.2
  275.2 2.4 broadcast_multiply_fusion.2
  286.7 2.4 broadcast_multiply_fusion.2
  296.0 1.9 copy.81
  298.0 2.8 reshape.447
  300.8 23.8 %all_to_all.12 = bf16[64,2,2048]{2,1,0:T(2,128)(2,1)S(1)} all-to-all(bf16[64,2,2048]{2,1,0:T(2,128)(2,1)} %reshape.447), channel_id=1, replica_groups=mesh['ctx'=64,'tp'=4] {'ctx'}, dimensions={0} | all-to-all | bytes 1048576 | tf_op jit(solution)/shard_map/all_to_all | solution.py:102
  324.6 7.1 %reshape.448 = bf16[8192,1,32]{2,1,0:T(2,128)(2,1)} reshape(bf16[64,2,2048]{2,1,0:T(2,128)(2,1)S(1)} %all_to_all.12) | data formatting | bytes 1048576
  331.8 8.0 %copy.74 = bf16[8192,1,32]{0,2,1:T(8,128)(2,1)S(1)} copy(bf16[8192,1,32]{2,1,0:T(2,128)(2,1)} %reshape.448) | data formatting | bytes 1048576 | tf_op jit(solution)/shard_map/all_to_all | solution.py:102
  341.3 9.6 %fusion.25 = f32[128,4096]{1,0:T(8,128)} fusion(bf16[1,2048,4096]{2,1,0:T(8,128)(2,1)} %all-gather.5.cloned.1.call-done, f32[128,1,2048]{0,2,1:T(8,128)S(1)} %get-tuple-element.150, f32[2048]{0:T(1024)S(1)} %bitcast.173, f32[128]{0:T(128)S(1)} %add_rsqrt_fusion), kind=kOutput, calls=%fused_computation.38 | convolution fusion | flops 2148270080 | bytes 19931648 | tf_op jit(solution)/shard_map/tgr,grd->td/dot_general | solution.py:109
  350.9 28.7 %reduce-scatter.2.cloned.1.call-done = f32[128,1024]{1,0:T(8,128)} async-done(((f32[128,4096]{1,0:T(8,128)}), f32[128,1024]{1,0:T(8,128)}) %reduce-scatter.2.cloned.1.call-update) | async-done | bytes 524304 | tf_op jit(solution)/shard_map/reduce_scatter | solution.py:115
  (287 shorter events, 141.2 us)
Async XLA Ops:
  6.5 49.0 %copy-start = (f32[1,32]{1,0:T(1,128)S(1)}, f32[1,32]{1,0:T(1,128)}, u32[]{:S(2)}) copy-start(f32[1,32]{1,0:T(1,128)} %param.13) | copy-start | bytes 388
  6.5 6.4 %copy-start.5 = (f32[1,4,2560]{2,1,0:T(4,128)S(1)}, f32[1,4,2560]{2,1,0:T(4,128)}, u32[]{:S(2)}) copy-start(f32[1,4,2560]{2,1,0:T(4,128)} %param.11) | copy-start | bytes 122884
  6.5 6.5 %slice-start = ((bf16[128,1,4640]{0,2,1:T(8,128)(2,1)}), bf16[128,1,2560]{0,2,1:T(8,128)(2,1)S(1)}, s32[]{:S(2)}) async-start(bf16[128,1,4640]{0,2,1:T(8,128)(2,1)} %param.10), calls=%async_computation.7 | async-start | bytes 1310720 | tf_op jit(solution)/shard_map/slice | solution.py:64
  6.5 97.2 %all-gather.3.cloned.1.call-start = ((), (), s32[]{:S(2)}) async-start(), calls=%async_computation.4 | async-start | bytes 8519680 | tf_op jit(solution)/shard_map/all_gather | solution.py:87
  8.2 5.1 %copy-start.6 = (f32[1,2560]{1,0:T(1,128)S(1)}, f32[1,2560]{1,0:T(1,128)}, u32[]{:S(2)}) copy-start(f32[1,2560]{1,0:T(1,128)} %param.12) | copy-start | bytes 30724
  8.2 5.6 %collective-permute-start = (bf16[3,1,2560]{2,0,1:T(4,128)(2,1)S(1)}, bf16[3,1,2560]{2,0,1:T(4,128)(2,1)S(1)}, u32[]{:S(2)}, u32[]{:S(2)}) collective-permute-start(bf16[3,1,2560]{2,0,1:T(4,128)(2,1)S(1)} %copy.77), channel_id=1, source_target_pairs={{0,4},{4,8},{8,12},{12,16},{16,20},{20,24},{24,28},{28,32},{32,36}... | collective-permute-start | bytes 46088 | tf_op jit(solution)/shard_map/ppermute | solution.py:19
  14.0 1.6 copy-start.7
  14.0 1.6 copy-start.2
  16.9 27.3 %all-to-all-start = ((bf16[128,1,64]{0,1,2:T(2,128)(2,1)}), bf16[128,1,64]{0,1,2:T(2,128)(2,1)S(1)}, u32[]{:S(2)}, u32[]{:S(2)}) async-start(bf16[128,1,64]{0,1,2:T(2,128)(2,1)} %copy.66), calls=%async_computation | async-start | bytes 65536 | tf_op jit(solution)/shard_map/all_to_all | solution.py:85
  43.2 13.0 %copy-start.8 = (f32[1,32]{1,0:T(1,128)S(1)}, f32[1,32]{1,0:T(1,128)}, u32[]{:S(2)}) copy-start(f32[1,32]{1,0:T(1,128)} %param.14) | copy-start | bytes 388
  44.2 28.2 %all-to-all-start.1 = ((bf16[64,2,2048]{2,1,0:T(2,128)(2,1)}), bf16[64,2,2048]{2,1,0:T(2,128)(2,1)S(1)}, u32[]{:S(2)}, u32[]{:S(2)}) async-start(bf16[64,2,2048]{2,1,0:T(2,128)(2,1)} %reshape.445), calls=%async_computation.1 | async-start | bytes 1048576 | tf_op jit(solution)/shard_map/all_to_all | solution.py:84
  54.5 286.5 %all-gather.5.cloned.1.call-start = ((), (), s32[]{:S(2)}) async-start(), calls=%async_computation.5 | async-start | bytes 17039360 | tf_op jit(solution)/shard_map/all_gather | solution.py:112
  55.3 324.3 %reduce-scatter.2.cloned.1.call-start = ((), (), s32[]{:S(2)}) async-start(), calls=%async_computation.6 | async-start | bytes 2621440 | tf_op jit(solution)/shard_map/reduce_scatter | solution.py:115
  76.8 32.8 %copy-start.3 = (bf16[16,512,1,32]{1,3,2,0:T(8,128)(2,1)S(1)}, bf16[16,512,1,32]{1,3,2,0:T(8,128)(2,1)}, u32[]{:S(2)}) copy-start(bf16[16,512,1,32]{1,3,2,0:T(8,128)(2,1)} %custom-call.3) | copy-start | bytes 1572868
  340.6 0.7 copy-start.4
  350.9 30.5 %copy-start.1 = (f32[1,32]{1,0:T(1,128)S(1)}, f32[1,32]{1,0:T(1,128)}, u32[]{:S(2)}) copy-start(f32[1,32]{1,0:T(1,128)} %param.13) | copy-start | bytes 388
Sparse Core Ops, SparseCore 0:
  15.7 87.9 all-gather.2
  106.5 97.1 all-gather.4
  351.1 28.4 reduce-scatter.1
where the time goes:
time: 391 us; the launch traced here: 388 us
  matrix products  91.8 us (23%)
  other arithmetic  75.4 us (19%)
  waiting for transfers between devices  71.7 us (18%)
  local copies, waits for them, and re-layouts  60.7 us (16%)
  starting transfers between devices  28.7 us (7%)
  blocking collectives  23.8 us (6%)
  loops' own time  22.3 us (6%)
  between operations  13.4 us (3%)
    mul x16, other arithmetic, advance(): weighted = x_block * tail_weight[:, :, None]  38.7 us
    reduce_scatter x1, waiting for transfers between devices, on_device(): shares = lax.psum_scatter(summed, 'tp', scatter_dimension=1, tiled=True)  28.7 us
    all_gather x1, waiting for transfers between devices, on_device(): all_keys = lax.all_gather(key_rows, 'ctx', axis=0, tiled=True)  26.9 us
    all_to_all x1, blocking collectives, on_device(): lax.all_to_all(jnp.stack(pieces_out, axis=1), 'ctx', split_axis=0, concat...  23.8 us
    another operation x1, loops' own time, ssd_blocks(): lax.scan(advance, initial, (x_blocks, step_blocks, b_blocks, c_blocks))  22.3 us
    dot_general x16, matrix products, advance(): jnp.dot(c_block, b_block.T, preferred_element_type=jnp.float32)  22 us
    dot_general x16, matrix products, advance(): jnp.einsum('shp,sn->hpn', weighted, b_float, precision=highest_precision)  21.3 us
    dot_general x16, matrix products, advance(): jnp.einsum('tn,hpn->thp', c_float, carried, precision=highest_precision)  20.8 us
  transfers between devices with their start and end apart: 6, of which 4 were waited for; matrix products, arithmetic and copies ran while one was open for 55% of the time, Pallas kernels for 0%

commit v1 on v0

--- a/solution.py
+++ b/solution.py
@@ -99,8 +99,14 @@
         4 * SPAN,
     )
     pieces_out = [outputs.reshape(sequence, shard_width).astype(jnp.bfloat16)]
-    scanned = lax.all_to_all(
-        jnp.stack(pieces_out, axis=1), "ctx", split_axis=0, concat_axis=2, tiled=True
+    scanned = jnp.concatenate(
+        lax.all_to_all(
+            jnp.stack(jnp.split(jnp.stack(pieces_out, axis=1), lax.axis_size("ctx"), axis=0)),
+            "ctx",
+            0,
+            0,
+        ),
+        axis=2,
     )
     gated = scanned.astype(jnp.float32) * jax.nn.silu(projected[:, :, :GCH].astype(jnp.float32))
     normed = (

time: 391 us -> 368 us (0.941)
  local copies, waits for them, and re-layouts: 60.7 us -> 41.7 us
    unnamed x27 -> x83, local copies, waits for them, and re-layouts: 14.9 us -> 4.8 us
    all_to_all x1 -> x0, local copies, waits for them, and re-layouts: 7.97 us -> none  [on_device(): lax.all_to_all(jnp.stack(pieces_out, axis=1), 'ctx', split_axis=0, concat...]
    unnamed x4 -> x3, other arithmetic: 11.6 us -> 11.5 us
  transfers between devices with their start and end apart: 6 -> 6, of which waited for: 4 -> 4; matrix products, arithmetic and copies ran while one was open for 55% -> 53% of each run, Pallas kernels for 0% -> 0%
where the time goes in v1:
time: 368 us; the launch traced here: 366 us
  matrix products  91.7 us (25%)
  other arithmetic  75.7 us (21%)
  waiting for transfers between devices  69.3 us (19%)
  local copies, waits for them, and re-layouts  41.7 us (11%)
  starting transfers between devices  28.7 us (8%)
  blocking collectives  23.8 us (6%)
  loops' own time  21.3 us (6%)
  between operations  13.6 us (4%)
    mul x16, other arithmetic, advance(): weighted = x_block * tail_weight[:, :, None]  38.7 us
    reduce_scatter x1, waiting for transfers between devices, on_device(): shares = lax.psum_scatter(summed, 'tp', scatter_dimension=1, tiled=True)  28.6 us
    all_gather x1, waiting for transfers between devices, on_device(): all_keys = lax.all_gather(key_rows, 'ctx', axis=0, tiled=True)  24.7 us
    all_to_all x1, blocking collectives, on_device(): lax.all_to_all(jnp.stack(jnp.split(jnp.stack(pieces_out, axis=1), lax.axi...  23.8 us
    dot_general x16, matrix products, advance(): jnp.dot(c_block, b_block.T, preferred_element_type=jnp.float32)  22 us
    another operation x1, loops' own time, ssd_blocks(): lax.scan(advance, initial, (x_blocks, step_blocks, b_blocks, c_blocks))  21.3 us
    dot_general x16, matrix products, advance(): jnp.einsum('shp,sn->hpn', weighted, b_float, precision=highest_precision)  21.2 us
    dot_general x16, matrix products, advance(): jnp.einsum('tn,hpn->thp', c_float, carried, precision=highest_precision)  20.7 us
  transfers between devices with their start and end apart: 6, of which 4 were waited for; matrix products, arithmetic and copies ran while one was open for 53% of the time, Pallas kernels for 0%

profile of v1, /device:TPU:1, one launch (start us, length us, event | category | flops | bytes accessed | tf_op | source)
XLA Modules:
  0.0 365.8 jit_solution(17066085548915860691)
XLA Ops:
  6.5 1.4 slice.126
  8.2 4.7 %collective-permute-start = (bf16[3,1,2560]{2,0,1:T(4,128)(2,1)S(1)}, bf16[3,1,2560]{2,0,1:T(4,128)(2,1)S(1)}, u32[]{:S(2)}, u32[]{:S(2)}) collective-permute-start(bf16[3,1,2560]{2,0,1:T(4,128)(2,1)S(1)} %copy.121), channel_id=1, source_target_pairs={{0,4},{4,8},{8,12},{12,16},{16,20},{20,24},{24,28},{28,32},{32,36}... | collective-permute-start | bytes 46088 | tf_op jit(solution)/shard_map/ppermute | solution.py:19
  16.9 13.5 %all-to-all-start = ((bf16[128,1,64]{0,1,2:T(2,128)(2,1)}), bf16[128,1,64]{0,1,2:T(2,128)(2,1)S(1)}, u32[]{:S(2)}, u32[]{:S(2)}) async-start(bf16[128,1,64]{0,1,2:T(2,128)(2,1)} %copy.113), calls=%async_computation | async-start | bytes 65536 | tf_op jit(solution)/shard_map/all_to_all | solution.py:85
  31.7 11.5 %reduce.12 = bf16[2048,128]{1,0:T(8,128)(2,1)S(1)} reduce(bf16[2048,1,128]{2,1,0:T(2,128)(2,1)S(1)} %bitcast.414, bf16[]{:T(256)} %broadcast.159), dimensions={1}, to_apply=%bitcast.348.reduce_sub_computation | reduce | bytes 1048578
  44.2 10.3 %all-to-all-start.1 = ((bf16[64,2,2048]{2,1,0:T(2,128)(2,1)}), bf16[64,2,2048]{2,1,0:T(2,128)(2,1)S(1)}, u32[]{:S(2)}, u32[]{:S(2)}) async-start(bf16[64,2,2048]{2,1,0:T(2,128)(2,1)} %reshape.562), calls=%async_computation.1 | async-start | bytes 1048576 | tf_op jit(solution)/shard_map/all_to_all | solution.py:84
  57.5 14.8 %all-to-all-done.1 = bf16[64,2,2048]{2,1,0:T(2,128)(2,1)S(1)} async-done(((bf16[64,2,2048]{2,1,0:T(2,128)(2,1)}), bf16[64,2,2048]{2,1,0:T(2,128)(2,1)S(1)}, u32[]{:S(2)}, u32[]{:S(2)}) %all-to-all-start.1) | async-done | bytes 524320 | tf_op jit(solution)/shard_map/all_to_all | solution.py:84
  72.3 1.8 reshape.563
  74.2 2.2 bitcast_convert_fusion
  76.3 2.7 copy.117
  79.0 24.7 %all-gather.3.cloned.1.call-done = bf16[8192,1,512]{2,0,1:T(8,128)(2,1)} async-done(((bf16[128,1,512]{2,0,1:T(8,128)(2,1)}), bf16[8192,1,512]{2,0,1:T(8,128)(2,1)}) %all-gather.3.cloned.1.call-update) | async-done | bytes 8388624 | tf_op jit(solution)/shard_map/all_gather | solution.py:87
  103.7 5.9 %fusion.41 = (bf16[8192,1,256]{2,0,1:T(8,128)(2,1)}, bf16[8192,1,256]{2,0,1:T(8,128)(2,1)}) fusion(bf16[8192,1,512]{2,0,1:T(8,128)(2,1)} %all-gather.3.cloned.1.call-done), kind=kLoop, calls=%fused_computation.202 | loop fusion | bytes 16777216 | tf_op jit(solution)/shard_map/slice | solution.py:98
  109.6 184.2 %while.14 = (s32[]{:T(128)}, f32[1,32,256]{2,1,0:T(8,128)S(1)}, bf16[16,512,1,32]{1,3,2,0:T(8,128)(2,1)S(1)}, f32[16,512,1]{1,0,2:T(8,128)S(1)}, f32[1]{0:T(128)...) while((s32[]{:T(128)}, f32[1,32,256]{2,1,0:T(8,128)S(1)}, ...), condition=%wide.region_3.4_spmd.clone.clone, body=%wide.region_0.0_spmd.clone.clone.sunk | while | flops 337266176 | bytes 4002620 | solution.py:57
  113.4 2.4 broadcast_multiply_fusion.2
  124.9 2.4 broadcast_multiply_fusion.2
  136.4 2.4 broadcast_multiply_fusion.2
  147.9 2.4 broadcast_multiply_fusion.2
  159.5 2.4 broadcast_multiply_fusion.2
  171.1 2.4 broadcast_multiply_fusion.2
  182.6 2.4 broadcast_multiply_fusion.2
  194.1 2.4 broadcast_multiply_fusion.2
  205.6 2.4 broadcast_multiply_fusion.2
  217.1 2.4 broadcast_multiply_fusion.2
  228.6 2.4 broadcast_multiply_fusion.2
  240.1 2.4 broadcast_multiply_fusion.2
  251.6 2.4 broadcast_multiply_fusion.2
  263.1 2.4 broadcast_multiply_fusion.2
  274.6 2.4 broadcast_multiply_fusion.2
  286.1 2.4 broadcast_multiply_fusion.2
  294.8 23.8 %all_to_all.23 = bf16[64,128,1,32]{1,3,2,0:T(8,128)(2,1)S(1)} all-to-all(bf16[64,128,1,32]{1,3,2,0:T(8,128)(2,1)S(1)} %constant_dynamic-update-slice_fusion), channel_id=1, replica_groups=mesh['ctx'=64,'tp'=4] {'ctx'}, dimensions={0} | all-to-all | bytes 1048576 | tf_op jit(solution)/shard_map/all_to_all | solution.py:103
  319.3 9.6 %fusion.25 = f32[128,4096]{1,0:T(8,128)} fusion(bf16[1,2048,4096]{2,1,0:T(8,128)(2,1)} %all-gather.5.cloned.1.call-done, f32[2048]{0:T(1024)S(1)} %bitcast.486, f32[128]{0:T(128)S(1)} %add_rsqrt_fusion, f32[128,1,2048]{0,2,1:T(8,128)S(1)} %bitcast.409, bf16[128,1,4640]{0,2,1:T(8,128)(2,1)S(1)} %copy-done.1), kind=kOutput, calls=%fused_computation.38 | convolution fusion | flops 2149842944 | bytes 20455936 | tf_op jit(solution)/shard_map/tgr,grd->td/dot_general | solution.py:115
  328.9 28.6 %reduce-scatter.2.cloned.1.call-done = f32[128,1024]{1,0:T(8,128)} async-done(((f32[128,4096]{1,0:T(8,128)}), f32[128,1024]{1,0:T(8,128)}) %reduce-scatter.2.cloned.1.call-update) | async-done | bytes 524304 | tf_op jit(solution)/shard_map/reduce_scatter | solution.py:121
  357.5 1.8 convert_element_type.96
  (340 shorter events, 135.0 us)
Async XLA Ops:
  6.5 49.0 %copy-start = (f32[1,32]{1,0:T(1,128)S(1)}, f32[1,32]{1,0:T(1,128)}, u32[]{:S(2)}) copy-start(f32[1,32]{1,0:T(1,128)} %param.13) | copy-start | bytes 388
  6.5 6.4 %copy-start.3 = (f32[1,4,2560]{2,1,0:T(4,128)S(1)}, f32[1,4,2560]{2,1,0:T(4,128)}, u32[]{:S(2)}) copy-start(f32[1,4,2560]{2,1,0:T(4,128)} %param.11) | copy-start | bytes 122884
  6.5 6.5 %slice-start = ((bf16[128,1,4640]{0,2,1:T(8,128)(2,1)}), bf16[128,1,2560]{0,2,1:T(8,128)(2,1)S(1)}, s32[]{:S(2)}) async-start(bf16[128,1,4640]{0,2,1:T(8,128)(2,1)} %param.10), calls=%async_computation.7 | async-start | bytes 1310720 | tf_op jit(solution)/shard_map/slice | solution.py:64
  6.5 97.2 %all-gather.3.cloned.1.call-start = ((), (), s32[]{:S(2)}) async-start(), calls=%async_computation.4 | async-start | bytes 8519680 | tf_op jit(solution)/shard_map/all_gather | solution.py:87
  8.2 5.1 %copy-start.4 = (f32[1,2560]{1,0:T(1,128)S(1)}, f32[1,2560]{1,0:T(1,128)}, u32[]{:S(2)}) copy-start(f32[1,2560]{1,0:T(1,128)} %param.12) | copy-start | bytes 30724
  8.2 5.6 %collective-permute-start = (bf16[3,1,2560]{2,0,1:T(4,128)(2,1)S(1)}, bf16[3,1,2560]{2,0,1:T(4,128)(2,1)S(1)}, u32[]{:S(2)}, u32[]{:S(2)}) collective-permute-start(bf16[3,1,2560]{2,0,1:T(4,128)(2,1)S(1)} %copy.121), channel_id=1, source_target_pairs={{0,4},{4,8},{8,12},{12,16},{16,20},{20,24},{24,28},{28,32},{32,36}... | collective-permute-start | bytes 46088 | tf_op jit(solution)/shard_map/ppermute | solution.py:19
  14.0 1.6 copy-start.5
  14.0 1.6 copy-start.1
  16.9 27.3 %all-to-all-start = ((bf16[128,1,64]{0,1,2:T(2,128)(2,1)}), bf16[128,1,64]{0,1,2:T(2,128)(2,1)S(1)}, u32[]{:S(2)}, u32[]{:S(2)}) async-start(bf16[128,1,64]{0,1,2:T(2,128)(2,1)} %copy.113), calls=%async_computation | async-start | bytes 65536 | tf_op jit(solution)/shard_map/all_to_all | solution.py:85
  43.2 13.0 %copy-start.6 = (f32[1,32]{1,0:T(1,128)S(1)}, f32[1,32]{1,0:T(1,128)}, u32[]{:S(2)}) copy-start(f32[1,32]{1,0:T(1,128)} %param.14) | copy-start | bytes 388
  44.2 28.1 %all-to-all-start.1 = ((bf16[64,2,2048]{2,1,0:T(2,128)(2,1)}), bf16[64,2,2048]{2,1,0:T(2,128)(2,1)S(1)}, u32[]{:S(2)}, u32[]{:S(2)}) async-start(bf16[64,2,2048]{2,1,0:T(2,128)(2,1)} %reshape.562), calls=%async_computation.1 | async-start | bytes 1048576 | tf_op jit(solution)/shard_map/all_to_all | solution.py:84
  54.5 264.6 %all-gather.5.cloned.1.call-start = ((), (), s32[]{:S(2)}) async-start(), calls=%async_computation.5 | async-start | bytes 17039360 | tf_op jit(solution)/shard_map/all_gather | solution.py:118
  55.3 302.2 %reduce-scatter.2.cloned.1.call-start = ((), (), s32[]{:S(2)}) async-start(), calls=%async_computation.6 | async-start | bytes 2621440 | tf_op jit(solution)/shard_map/reduce_scatter | solution.py:121
  318.6 0.7 copy-start.2
Sparse Core Ops, SparseCore 0:
  15.7 87.9 all-gather.2
  106.5 96.9 all-gather.4
  329.1 28.4 reduce-scatter.1
